TPU v7x, 32 devices: a whole 2x2x4 slice. The times are simulated.
32 devices in a mesh: grp: 2 (over y), seq: 4 (over z), outer: 4 (over x, core).
Axes of the slice: x: 2, y: 2, z: 4, core: 2. Of those that a mesh axis runs over, the one named last changes fastest.
Arguments:
- inputs: bfloat16 [32768, 512], P(('grp', 'outer', 'seq')), parts along dimension 0, may hold values from -6 to 6
- grad_out: bfloat16 [32768, 512], P(('grp', 'outer', 'seq')), parts along dimension 0, may hold values from -6 to 6
- w_query: bfloat16 [512, 512], replicated, may hold values from -0.25 to 0.25
- w_key: bfloat16 [512, 512], replicated, may hold values from -0.25 to 0.25
- w_value: bfloat16 [512, 512], replicated, may hold values from -0.25 to 0.25
- conv_taps: bfloat16 [4, 512], replicated, may hold values from -3 to 3
Outputs:
- grad_inputs: bfloat16 [32768, 512], P(('grp', 'outer', 'seq')), parts along dimension 0
- grad_wq: float32 [1024, 512], P('grp'), parts along dimension 0
- grad_wk: float32 [1024, 512], P('grp'), parts along dimension 0
- grad_wv: float32 [1024, 512], P('grp'), parts along dimension 0
- grad_conv: float32 [8, 512], P('grp'), parts along dimension 0
There are 2 independent parts, one for each index of `grp`. A program takes and returns all parts, laid end to end along the dimension named above; an argument that names none is the same for every part. Nothing has to cross between parts.
All inputs are finite; a program needn't handle non-finite values.
Results may differ from a plain program's by a relative error of at most 0.0095.
Values may be sent and summed in bfloat16 or wider, within the bound.
A program may use at most 128 MiB of HBM per device.

v0:
```python
import math
import jax
import jax.numpy as jnp
from jax import lax
from jax.sharding import PartitionSpec as P

D = 512
HEADS = 8
HEAD_DIM = 64
TAPS = 4
BLOCK = 512


def shifted(x, axis, by):
    devices = lax.axis_size(axis)
    return lax.ppermute(x, axis, [(i, (i + by) % devices) for i in range(devices)])


def from_behind(value, axis, steps):
    count = lax.axis_size(axis)
    leading, last = (max(0, -steps), min(count, count - steps))
    return lax.ppermute(value, axis, [(source, source + steps) for source in range(leading, last)])


def entering(x, axis, join, neutral, backward):
    count = lax.axis_size(axis)
    place = lax.axis_index(axis)
    ahead = count - 1 - place if backward else place
    gathered = lax.all_gather(x.astype(jnp.bfloat16), axis)
    state = jnp.zeros_like(x) + jnp.asarray(neutral, x.dtype)

    def one(step, state):
        source = count - 1 - step if backward else step
        return join(state, lax.dynamic_index_in_dim(gathered, source, 0, False).astype(x.dtype))

    return lax.fori_loop(0, ahead, one, state)


def add_states(earlier, later):
    return earlier + later


def block_grads(parts):
    queries, key_rows, value_rows, grad_rows, scales, state_prev, state_next = parts
    size = queries.shape[0]
    highest = lax.Precision.HIGHEST
    causal = lax.broadcasted_iota(jnp.int32, (size, size), 0) >= lax.broadcasted_iota(
        jnp.int32, (size, size), 1
    )
    scores = jnp.einsum("thj,shj->hts", grad_rows, value_rows, preferred_element_type=jnp.float32)
    probe = jnp.where(causal[None], scores * scales[None, :, None], 0.0).astype(jnp.bfloat16)
    grad_query = jnp.einsum("hts,shi->thi", probe, key_rows, preferred_element_type=jnp.float32)
    grad_query = grad_query + scales[:, None, None] * jnp.einsum(
        "thj,hij->thi", grad_rows.astype(jnp.float32), state_prev, precision=highest
    )
    grad_key = jnp.einsum("hts,thi->shi", probe, queries, preferred_element_type=jnp.float32)
    grad_key = grad_key + jnp.einsum(
        "shj,hij->shi", value_rows.astype(jnp.float32), state_next, precision=highest
    )
    affinity = jnp.einsum("thi,shi->hts", queries, key_rows, preferred_element_type=jnp.float32)
    mixing = jnp.where(causal[None], affinity * scales[None, :, None], 0.0).astype(jnp.bfloat16)
    grad_value = jnp.einsum("hts,thj->shj", mixing, grad_rows, preferred_element_type=jnp.float32)
    grad_value = grad_value + jnp.einsum(
        "shi,hij->shj", key_rows.astype(jnp.float32), state_next, precision=highest
    )
    return (
        grad_query.reshape(size, D).astype(jnp.bfloat16),
        grad_key.reshape(size, D).astype(jnp.bfloat16),
        grad_value.reshape(size, D).astype(jnp.bfloat16),
    )


def on_device(inputs, grad_out, w_query, w_key, w_value, conv_taps):
    length = inputs.shape[0]
    model_width = inputs.shape[1]
    highest = lax.Precision.HIGHEST
    seq_count = lax.axis_size("seq")
    seq_place = lax.axis_index("seq")
    outer_place = lax.axis_index("outer")
    offset = (outer_place * seq_count + seq_place) * length
    queries = jnp.dot(inputs, w_query, preferred_element_type=jnp.float32).astype(jnp.bfloat16)
    keys_pre = jnp.dot(inputs, w_key, preferred_element_type=jnp.float32).astype(jnp.bfloat16)
    values = jnp.dot(inputs, w_value, preferred_element_type=jnp.float32).astype(jnp.bfloat16)
    tail_rows = keys_pre[length - (TAPS - 1) :]
    wrapped = shifted(tail_rows, "seq", 1)
    across = from_behind(wrapped, "outer", 1)
    before = jnp.where(seq_place == 0, across, wrapped)
    taps = conv_taps.astype(jnp.float32)
    padded = jnp.concatenate([before, keys_pre], 0).astype(jnp.float32)
    keys = jnp.zeros((length, model_width), jnp.float32)
    for tap_index in range(TAPS):
        keys = keys + taps[tap_index] * padded[TAPS - 1 - tap_index : TAPS - 1 - tap_index + length]
    keys = keys.astype(jnp.bfloat16)
    position = (offset + jnp.arange(length, dtype=jnp.int32)).astype(jnp.float32)
    scales = 1.0 / (jnp.sqrt(position + 1.0) * math.sqrt(HEAD_DIM))
    block_count = length // BLOCK
    shape = (block_count, BLOCK, HEADS, HEAD_DIM)
    query_heads = queries.reshape(shape)
    key_heads = keys.reshape(shape)
    value_heads = values.reshape(shape)
    grad_heads = grad_out.reshape(shape)
    block_scales = scales.reshape(block_count, BLOCK)
    kv_blocks = jnp.einsum(
        "nbhi,nbhj->nhij", key_heads, value_heads, preferred_element_type=jnp.float32
    )
    scaled_queries = query_heads.astype(jnp.float32) * block_scales[:, :, None, None]
    qdo_blocks = jnp.einsum(
        "nbhi,nbhj->nhij", scaled_queries, grad_heads.astype(jnp.float32), precision=highest
    )
    kv_local = jnp.sum(kv_blocks, 0)
    qdo_local = jnp.sum(qdo_blocks, 0)
    zeros = jnp.zeros_like(kv_local)
    kv_inner = entering(kv_local, "seq", add_states, zeros, False)
    kv_group, qdo_group = lax.psum((kv_local, qdo_local), "seq")
    kv_outer = entering(kv_group, "outer", add_states, zeros, False)
    qdo_inner = entering(qdo_local, "seq", add_states, zeros, True)
    qdo_outer = entering(qdo_group, "outer", add_states, zeros, True)
    state_before = kv_outer + kv_inner
    state_after = qdo_outer + qdo_inner
    state_prev = state_before[None] + jnp.cumsum(kv_blocks, 0) - kv_blocks
    state_next = state_after[None] + qdo_local[None] - jnp.cumsum(qdo_blocks, 0)
    grad_query, grad_key, grad_value = lax.map(
        block_grads,
        (query_heads, key_heads, value_heads, grad_heads, block_scales, state_prev, state_next),
    )
    grad_query = grad_query.reshape(length, model_width)
    grad_key = grad_key.reshape(length, model_width)
    grad_value = grad_value.reshape(length, model_width)
    head_rows = grad_key[: TAPS - 1]
    wrapped_back = shifted(head_rows, "seq", -1)
    across_back = from_behind(wrapped_back, "outer", -1)
    behind = jnp.where(seq_place == seq_count - 1, across_back, wrapped_back)
    key_grad32 = grad_key.astype(jnp.float32)
    extended = jnp.concatenate([grad_key, behind], 0).astype(jnp.float32)
    grad_pre = jnp.zeros((length, model_width), jnp.float32)
    tap_grads = []
    for tap_index in range(TAPS):
        grad_pre = grad_pre + taps[tap_index] * extended[tap_index : tap_index + length]
        tap_grads.append(
            jnp.sum(key_grad32 * padded[TAPS - 1 - tap_index : TAPS - 1 - tap_index + length], 0)
        )
    grad_pre = grad_pre.astype(jnp.bfloat16)
    conv_local = jnp.stack(tap_grads, 0)
    contract = (((1,), (1,)), ((), ()))
    grad_inputs = lax.dot_general(grad_query, w_query, contract, preferred_element_type=jnp.float32)
    grad_inputs = grad_inputs + lax.dot_general(
        grad_pre, w_key, contract, preferred_element_type=jnp.float32
    )
    grad_inputs = grad_inputs + lax.dot_general(
        grad_value, w_value, contract, preferred_element_type=jnp.float32
    )
    grad_inputs = grad_inputs.astype(jnp.bfloat16)
    over_rows = (((0,), (0,)), ((), ()))
    local_wq = lax.dot_general(inputs, grad_query, over_rows, preferred_element_type=jnp.float32)
    local_wk = lax.dot_general(inputs, grad_pre, over_rows, preferred_element_type=jnp.float32)
    local_wv = lax.dot_general(inputs, grad_value, over_rows, preferred_element_type=jnp.float32)
    grad_wq, grad_wk, grad_wv, grad_conv = lax.psum(
        (local_wq, local_wk, local_wv, conv_local), ("seq", "outer")
    )
    return (grad_inputs, grad_wq, grad_wk, grad_wv, grad_conv)


def solution(mesh):
    in_specs = (
        P(("grp", "outer", "seq"), None),
        P(("grp", "outer", "seq"), None),
        P(),
        P(),
        P(),
        P(),
    )
    out_specs = (
        P(("grp", "outer", "seq"), None),
        P("grp", None),
        P("grp", None),
        P("grp", None),
        P("grp", None),
    )
    return jax.shard_map(
        on_device, mesh=mesh, in_specs=in_specs, out_specs=out_specs, check_vma=False
    )
```

profile of v0, /device:TPU:0, one launch (start us, length us, event | category | flops | bytes accessed | tf_op | source)
XLA Modules:
  0.0 333.5 jit_solution(12223095739537456281)
XLA Ops:
  11.1 3.0 collective-permute-start
  16.2 2.5 copy.51
  26.5 15.4 %all-gather.3 = bf16[32,64,64]{2,1,0:T(8,128)(2,1)S(1)} all-gather(bf16[8,64,64]{2,1,0:T(8,128)(2,1)S(1)} %convert_element_type.173), channel_id=5, replica_groups=mesh['grp'=2,'seq'=4,'outer'=4] {'seq'}, dimensions={0}, use_global_device_ids=true | all-gather | bytes 327680 | tf_op jit(solution)/shard_map/all_gather | solution.py:29
  42.2 2.8 convolution_convert_fusion.1
  47.6 2.8 reshape.137
  50.4 2.2 copy.52
  56.1 3.9 %reshape.135 = bf16[2,512,8,64]{3,2,1,0:T(8,128)(2,1)} reshape(bf16[1024,512]{1,0:T(8,128)(2,1)} %add_convert_fusion.1) | data formatting | bytes 2097152 | tf_op jit(solution)/shard_map/reshape | solution.py:99
  60.0 3.3 copy.50
  63.3 2.8 fusion.63
  66.8 16.7 %all-gather.1 = bf16[32,64,64]{2,1,0:T(8,128)(2,1)} all-gather(bf16[8,64,64]{2,1,0:T(8,128)(2,1)S(1)} %convert_element_type.168), channel_id=3, replica_groups=mesh['grp'=2,'seq'=4,'outer'=4] {'seq'}, dimensions={0}, use_global_device_ids=true | all-gather | bytes 327680 | tf_op jit(solution)/shard_map/all_gather | solution.py:29
  83.5 29.6 %all-reduce.6 = (bf16[8,64,64]{2,1,0:T(8,128)(2,1)}, bf16[8,64,64]{2,1,0:T(8,128)(2,1)S(1)}) all-reduce(f32[8,64,64]{2,1,0:T(8,128)} %copy-done.16, f32[8,64,64]{2,1,0:T(8,128)S(1)} %get-tuple-element.348), channel_id=1, replica_groups=mesh['grp'=2,'seq'=4,'outer'=4] {'seq'}, use_global_device_ids=true, to_apply=%region_1.2 | all-reduce | flops 65536 | bytes 393216 | tf_op jit(solution)/shard_map/psum | solution.py:114
  113.2 7.2 %all-gather = bf16[32,64,64]{2,1,0:T(8,128)(2,1)} all-gather(bf16[8,64,64]{2,1,0:T(8,128)(2,1)} %get-tuple-element.338), channel_id=2, replica_groups=mesh['grp'=2,'seq'=4,'outer'=4] {'outer'}, dimensions={0}, use_global_device_ids=true | all-gather | bytes 327680 | tf_op jit(solution)/shard_map/all_gather | solution.py:29
  121.1 10.4 %all-gather.2 = bf16[32,64,64]{2,1,0:T(8,128)(2,1)} all-gather(bf16[8,64,64]{2,1,0:T(8,128)(2,1)S(1)} %get-tuple-element.339), channel_id=4, replica_groups=mesh['grp'=2,'seq'=4,'outer'=4] {'outer'}, dimensions={0}, use_global_device_ids=true | all-gather | bytes 327680 | tf_op jit(solution)/shard_map/all_gather | solution.py:29
  132.2 5.1 %while.60 = (s32[]{:T(128)}, f32[8,64,64]{2,1,0:T(8,128)}, s32[]{:T(128)}, bf16[4,8,64,64]{3,2,1,0:T(8,128)(2,1)}, s32[]{:T(128)}, /*index=5*/s32[]{:T(128)}, s32[]{:T(128)}, s32[]{:T(128)}) while((s32[]{:T(128)}, f32[8,64,64]{2,1,0:T(8,128)}, s32[]{:T(128)}, bf16[4,8,64,64]{3,2,1,0:T(8,128)(2,1)}, s32[]{:T(128)}, /*index=5*/s32[]{:T(128)}, ...), condition=%wide.region_10.11_spmd, body=%wide.region_9.10_spmd.sunk | while | flops 65542 | bytes 327823 | solution.py:36
  138.5 2.2 fusion.61
  141.6 59.3 %while.62 = (s32[]{:T(128)}, bf16[2,512,512]{2,1,0:T(8,128)(2,1)}, bf16[2,512,512]{2,1,0:T(8,128)(2,1)}, bf16[2,512,512]{2,1,0:T(8,128)(2,1)}, bf16[2,512,8,64]{...) while((s32[]{:T(128)}, bf16[2,512,512]{2,1,0:T(8,128)(2,1)}, ...), condition=%wide.region_15.16_spmd, body=%wide.region_14.15_spmd.sunk | while | flops 1960837120 | bytes 65027896 | solution.py:122
  141.7 3.0 select_convert_fusion.6
  152.6 4.6 %fusion.130 = f32[8,64,512]{2,1,0:T(8,128)} fusion(f32[512]{0:T(512)S(1)} %bitcast.174, pred[512,512]{1,0:T(8,128)(4,1)S(1)} %iota_compare_fusion.2, bf16[2,512,8,64]{1,3,2,0:T(8,128)(2,1)} %get-tuple-element.648, s32[]{:T(128)S(6)} %copy.116, bf16[2,512,8,64]{1,3,2,0:T(8,128)(2,1)} %get-tuple-element.644, bf16[2,512,8,64]{1,3,2,0:T(8,128)(2,1)} %get-tuple-element.643), kind=kOutput, calls=%fused_computation.6.clone.1 | convolution fusion | flops 543162368 | bytes 2887168 | tf_op jit(solution)/shard_map/while/body/eval_jaxpr/hts,thj->shj/dot_general | solution.py:62
  157.2 2.9 fusion.131
  162.2 3.3 fusion.132
  169.0 2.2 constant_dynamic-update-slice_fusion.6
  171.3 3.0 select_convert_fusion.6
  182.3 4.6 %fusion.130 = f32[8,64,512]{2,1,0:T(8,128)} fusion(f32[512]{0:T(512)S(1)} %bitcast.174, pred[512,512]{1,0:T(8,128)(4,1)S(1)} %iota_compare_fusion.2, bf16[2,512,8,64]{1,3,2,0:T(8,128)(2,1)} %get-tuple-element.648, s32[]{:T(128)S(6)} %copy.116, bf16[2,512,8,64]{1,3,2,0:T(8,128)(2,1)} %get-tuple-element.644, bf16[2,512,8,64]{1,3,2,0:T(8,128)(2,1)} %get-tuple-element.643), kind=kOutput, calls=%fused_computation.6.clone.1 | convolution fusion | flops 543162368 | bytes 2887168 | tf_op jit(solution)/shard_map/while/body/eval_jaxpr/hts,thj->shj/dot_general | solution.py:62
  186.9 2.9 fusion.131
  191.8 3.3 fusion.132
  198.7 2.2 constant_dynamic-update-slice_fusion.6
  201.6 5.2 %collective-permute-start.2 = (bf16[3,512]{1,0:T(4,128)(2,1)S(1)}, bf16[3,512]{1,0:T(4,128)(2,1)S(1)}, u32[]{:S(2)}, u32[]{:S(2)}) collective-permute-start(bf16[3,512]{1,0:T(4,128)(2,1)S(1)} %slice.73), channel_id=1, source_target_pairs={{0,12},{4,0},{8,4},{12,8},{1,13},{5,1},{9,5},{13,9},{2,14},{6,2},{... | collective-permute-start | bytes 9224 | tf_op jit(solution)/shard_map/ppermute | solution.py:16
  206.8 3.0 convolution_bitcast_fusion.2
  217.2 2.3 fusion.51
  219.5 32.9 %psum.47 = f32[4,512]{1,0:T(4,128)} all-reduce(f32[4,512]{1,0:T(4,128)S(1)} %pad_maximum_fusion), channel_id=1, replica_groups=mesh['grp'=2,'seq'=4,'outer'=4] {'seq','outer'}, use_global_device_ids=true, to_apply=%region_23.24 | all-reduce | flops 2048 | bytes 16384 | tf_op jit(solution)/shard_map/psum | solution.py:157
  257.6 63.7 %all-reduce.5.cloned.1.call-done = (f32[512,512]{0,1:T(8,128)}, f32[512,512]{0,1:T(8,128)}, f32[512,512]{0,1:T(8,128)}) async-done(((f32[512,512]{0,1:T(8,128)}, f32[512,512]{0,1:T(8,128)}, f32[512,512]{0,1:T(8,128)}), (f32[512,512]{0,1:T(8,128)}, f32[512,512]{0,1:T(8,128)}, f32[512,512]{0,1:T(8,128)})) %all-reduce.5.cloned.1.call-update) | async-done | bytes 3145744 | tf_op jit(solution)/shard_map/psum | solution.py:157
  321.4 2.7 copy.57
  (160 shorter events, 72.3 us)
Async XLA Ops:
  7.2 7.0 %copy-start.19 = (bf16[1024,512]{1,0:T(8,128)(2,1)S(1)}, bf16[1024,512]{1,0:T(8,128)(2,1)}, u32[]{:S(2)}) copy-start(bf16[1024,512]{1,0:T(8,128)(2,1)} %param.17) | copy-start | bytes 3145732
  7.2 314.2 %all-reduce.5.cloned.1.call-start = ((), (), s32[]{:S(2)}) async-start(), calls=%async_computation | async-start | bytes 6291456 | tf_op jit(solution)/shard_map/psum | solution.py:157
  11.1 33.9 %collective-permute-start = (bf16[3,512]{1,0:T(4,128)(2,1)S(1)}, bf16[3,512]{1,0:T(4,128)(2,1)S(1)}, u32[]{:S(2)}, u32[]{:S(2)}) collective-permute-start(bf16[3,512]{1,0:T(4,128)(2,1)S(1)} %slice.65), channel_id=1, source_target_pairs={{0,4},{4,8},{8,12},{12,0},{1,5},{5,9},{9,13},{13,1},{2,6},{6,10},{... | collective-permute-start | bytes 9224 | tf_op jit(solution)/shard_map/ppermute | solution.py:16
  18.7 5.6 %copy-start.3 = (bf16[2,512,8,64]{1,3,2,0:T(8,128)(2,1)}, bf16[2,512,8,64]{1,3,2,0:T(8,128)(2,1)S(1)}, u32[]{:S(2)}) copy-start(bf16[2,512,8,64]{1,3,2,0:T(8,128)(2,1)S(1)} %copy.51) | copy-start | bytes 3145732
  18.8 5.3 %copy-start.26 = (f32[2,512]{1,0:T(2,128)}, f32[2,512]{1,0:T(2,128)S(1)}, u32[]{:S(2)}) copy-start(f32[2,512]{1,0:T(2,128)S(1)} %multiply_divide_fusion) | copy-start | bytes 12292
  26.5 57.1 %copy-start.14 = (f32[8,64,64]{2,1,0:T(8,128)}, f32[8,64,64]{2,1,0:T(8,128)S(1)}, u32[]{:S(2)}) copy-start(f32[8,64,64]{2,1,0:T(8,128)S(1)} %get-tuple-element.348) | copy-start | bytes 393220
  42.2 5.4 %copy-start.8 = (f32[8,64,64]{2,1,0:T(8,128)}, f32[8,64,64]{2,1,0:T(8,128)S(1)}, u32[]{:S(2)}) copy-start(f32[8,64,64]{2,1,0:T(8,128)S(1)} %get-tuple-element.225) | copy-start | bytes 393220
  42.2 4.1 %copy-start.36 = (bf16[4,512]{1,0:T(4,128)(2,1)S(1)}, bf16[4,512]{1,0:T(4,128)(2,1)}, u32[]{:S(2)}) copy-start(bf16[4,512]{1,0:T(4,128)(2,1)} %param.21) | copy-start | bytes 12292
  45.0 7.6 %collective-permute-start.1 = (bf16[3,512]{1,0:T(4,128)(2,1)S(1)}, bf16[3,512]{1,0:T(4,128)(2,1)S(1)}, u32[]{:S(2)}, u32[]{:S(2)}) collective-permute-start(bf16[3,512]{1,0:T(4,128)(2,1)S(1)} %collective-permute-done), channel_id=1, source_target_pairs={{0,1},{1,2},{2,3},{4,5},{5,6},{6,7},{8,9},{9,10},{10,11},{12,13},{... | collective-permute-start | bytes 9224 | tf_op jit(solution)/shard_map/ppermute | solution.py:22
  46.3 7.8 %copy-start.28 = (f32[1,512]{1,0:T(1,128)}, f32[1,512]{1,0:T(1,128)S(1)}, u32[]{:S(2)}) copy-start(f32[1,512]{1,0:T(1,128)S(1)} %get-tuple-element.342) | copy-start | bytes 6148
  46.3 7.8 %copy-start.30 = (f32[1,512]{1,0:T(1,128)}, f32[1,512]{1,0:T(1,128)S(1)}, u32[]{:S(2)}) copy-start(f32[1,512]{1,0:T(1,128)S(1)} %get-tuple-element.343) | copy-start | bytes 6148
  46.4 7.8 %copy-start.32 = (f32[1,512]{1,0:T(1,128)}, f32[1,512]{1,0:T(1,128)S(1)}, u32[]{:S(2)}) copy-start(f32[1,512]{1,0:T(1,128)S(1)} %get-tuple-element.344) | copy-start | bytes 6148
  46.4 7.8 %copy-start.34 = (f32[1,512]{1,0:T(1,128)}, f32[1,512]{1,0:T(1,128)S(1)}, u32[]{:S(2)}) copy-start(f32[1,512]{1,0:T(1,128)S(1)} %get-tuple-element.345) | copy-start | bytes 6148
  137.4 3.3 copy-start.7
  137.4 3.3 copy-start.9
  137.4 3.3 copy-start.15
  137.4 3.4 %copy-start.17 = (f32[2,8,64,64]{3,2,1,0:T(8,128)S(1)}, f32[2,8,64,64]{3,2,1,0:T(8,128)}, u32[]{:S(2)}) copy-start(f32[2,8,64,64]{3,2,1,0:T(8,128)} %get-tuple-element.349) | copy-start | bytes 786436
  138.5 3.1 copy-start.27
  141.7 3.0 copy-start.2
  144.7 2.5 copy-start.10
  162.2 3.3 copy-start.5
  162.2 3.3 copy-start.6
  171.3 3.0 copy-start.2
  191.8 3.3 copy-start.5
  191.8 3.3 copy-start.6
  201.6 8.3 %collective-permute-start.2 = (bf16[3,512]{1,0:T(4,128)(2,1)S(1)}, bf16[3,512]{1,0:T(4,128)(2,1)S(1)}, u32[]{:S(2)}, u32[]{:S(2)}) collective-permute-start(bf16[3,512]{1,0:T(4,128)(2,1)S(1)} %slice.73), channel_id=1, source_target_pairs={{0,12},{4,0},{8,4},{12,8},{1,13},{5,1},{9,5},{13,9},{2,14},{6,2},{... | collective-permute-start | bytes 9224 | tf_op jit(solution)/shard_map/ppermute | solution.py:16
  206.8 4.3 %copy-start.22 = (bf16[2,512,512]{2,1,0:T(8,128)(2,1)S(1)}, bf16[2,512,512]{2,1,0:T(8,128)(2,1)}, u32[]{:S(2)}) copy-start(bf16[2,512,512]{2,1,0:T(8,128)(2,1)} %get-tuple-element.228) | copy-start | bytes 3145732
  209.8 3.0 collective-permute-start.3
  219.5 35.0 %copy-start.13 = (bf16[1024,512]{1,0:T(8,128)(2,1)S(1)}, bf16[1024,512]{1,0:T(8,128)(2,1)}, u32[]{:S(2)}) copy-start(bf16[1024,512]{1,0:T(8,128)(2,1)} %copy-done.12) | copy-start | bytes 3145732
  219.5 35.0 %copy-start.24 = (bf16[512,512]{1,0:T(8,128)(2,1)S(1)}, bf16[512,512]{1,0:T(8,128)(2,1)}, u32[]{:S(2)}) copy-start(bf16[512,512]{1,0:T(8,128)(2,1)} %param.19) | copy-start | bytes 1572868
  321.4 2.7 copy-start.21
  321.4 4.0 %copy-start.20 = (f32[512,512]{0,1:T(8,128)S(1)}, f32[512,512]{0,1:T(8,128)}, u32[]{:S(2)}) copy-start(f32[512,512]{0,1:T(8,128)} %get-tuple-element.337) | copy-start | bytes 3145732
  (16 other events, 21.6 us)
Sparse Core Ops, SparseCore 0:
  217.3 104.0 all-reduce.4
where the time goes:
time: 335 us; the launch traced here: 334 us
  blocking collectives  112 us (33%)
  waiting for transfers between devices  63.8 us (19%)
  matrix products  58.5 us (17%)
  local copies, waits for them, and re-layouts  56.5 us (17%)
  other arithmetic  16.9 us (5%)
  between operations  14.5 us (4%)
  starting transfers between devices  10.8 us (3%)
    psum x1, waiting for transfers between devices, on_device(): lax.psum((local_wq, local_wk, local_wv, conv_local), ('seq', 'outer'))  63.7 us
    all_gather x4, blocking collectives, entering(): gathered = lax.all_gather(x.astype(jnp.bfloat16), axis)  49.7 us
    psum x1, blocking collectives, on_device(): lax.psum((local_wq, local_wk, local_wv, conv_local), ('seq', 'outer'))  32.9 us
    psum x1, blocking collectives, on_device(): kv_group, qdo_group = lax.psum((kv_local, qdo_local), 'seq')  29.6 us
    dynamic_update_slice x10, local copies, waits for them, and re-layouts, on_device(): lax.map(block_grads, (query_heads, key_heads, value_heads, grad_heads, bl...  20.6 us
    unnamed x66, local copies, waits for them, and re-layouts  10.2 us
    dot_general x2, matrix products, block_grads(): jnp.einsum('hts,thj->shj', mixing, grad_rows, preferred_element_type=jnp....  9.25 us
    while x4, local copies, waits for them, and re-layouts, on_device(): lax.map(block_grads, (query_heads, key_heads, value_heads, grad_heads, bl...  9.23 us
  transfers between devices with their start and end apart: 5, of which 1 were waited for; matrix products, arithmetic and copies ran while one was open for 10% of the time, Pallas kernels for 0%

commit v1 on v0

--- a/solution.py
+++ b/solution.py
@@ -1,3 +1,4 @@
+import functools
 import math
 import jax
 import jax.numpy as jnp
@@ -9,6 +10,15 @@
 HEAD_DIM = 64
 TAPS = 4
 BLOCK = 512
+
+
+def lift_the_positions(message, device_axis, axis_key):
+    for jj in (device_axis, axis_key):
+        message = lax.psum(message, jj)
+    return message
+
+
+_work_sizes = functools.partial(lift_the_positions, device_axis="outer", axis_key="seq")
 
 
 def shifted(x, axis, by):
@@ -154,9 +164,7 @@
     local_wq = lax.dot_general(inputs, grad_query, over_rows, preferred_element_type=jnp.float32)
     local_wk = lax.dot_general(inputs, grad_pre, over_rows, preferred_element_type=jnp.float32)
     local_wv = lax.dot_general(inputs, grad_value, over_rows, preferred_element_type=jnp.float32)
-    grad_wq, grad_wk, grad_wv, grad_conv = lax.psum(
-        (local_wq, local_wk, local_wv, conv_local), ("seq", "outer")
-    )
+    grad_wq, grad_wk, grad_wv, grad_conv = _work_sizes((local_wq, local_wk, local_wv, conv_local))
     return (grad_inputs, grad_wq, grad_wk, grad_wv, grad_conv)
 
 

time: 335 us -> 425 us (1.27)
  waiting for transfers between devices: 63.8 us -> 166 us
  blocking collectives: 112 us -> 100 us
    psum x1 -> x2, waiting for transfers between devices: 63.7 us -> 166 us  [lift_the_positions(): message = lax.psum(message, jj)]
    psum x1 -> x2, blocking collectives: 32.9 us -> 19.3 us  [lift_the_positions(): message = lax.psum(message, jj)]
    unnamed x66 -> x62, local copies, waits for them, and re-layouts: 10.2 us -> 8.59 us
  transfers between devices with their start and end apart: 5 -> 6, of which waited for: 1 -> 2; matrix products, arithmetic and copies ran while one was open for 10% -> 8% of each run, Pallas kernels for 0% -> 0%
where the time goes in v1:
time: 425 us; the launch traced here: 424 us
  waiting for transfers between devices  166 us (39%)
  blocking collectives  100 us (24%)
  matrix products  60.1 us (14%)
  local copies, waits for them, and re-layouts  55 us (13%)
  other arithmetic  16.9 us (4%)
  between operations  14.5 us (3%)
  starting transfers between devices  10.9 us (3%)
    psum x2, waiting for transfers between devices, lift_the_positions(): message = lax.psum(message, jj)  166 us
    all_gather x4, blocking collectives, entering(): gathered = lax.all_gather(x.astype(jnp.bfloat16), axis)  49.9 us
    psum x1, blocking collectives, on_device(): kv_group, qdo_group = lax.psum((kv_local, qdo_local), 'seq')  30.7 us
    dynamic_update_slice x10, local copies, waits for them, and re-layouts, on_device(): lax.map(block_grads, (query_heads, key_heads, value_heads, grad_heads, bl...  20.7 us
    psum x2, blocking collectives, lift_the_positions(): message = lax.psum(message, jj)  19.3 us
    dot_general x2, matrix products, block_grads(): jnp.einsum('hts,thj->shj', mixing, grad_rows, preferred_element_type=jnp....  9.26 us
    while x4, local copies, waits for them, and re-layouts, on_device(): lax.map(block_grads, (query_heads, key_heads, value_heads, grad_heads, bl...  9.25 us
    unnamed x62, local copies, waits for them, and re-layouts  8.59 us
  transfers between devices with their start and end apart: 6, of which 2 were waited for; matrix products, arithmetic and copies ran while one was open for 8% of the time, Pallas kernels for 0%

profile of v1, /device:TPU:0, one launch (start us, length us, event | category | flops | bytes accessed | tf_op | source)
XLA Modules:
  0.0 423.6 jit_solution(4241667613498182519)
XLA Ops:
  10.2 3.1 collective-permute-start
  15.3 2.5 copy.51
  25.6 15.2 %all-gather.3 = bf16[32,64,64]{2,1,0:T(8,128)(2,1)S(1)} all-gather(bf16[8,64,64]{2,1,0:T(8,128)(2,1)S(1)} %convert_element_type.173), channel_id=5, replica_groups=mesh['grp'=2,'seq'=4,'outer'=4] {'seq'}, dimensions={0}, use_global_device_ids=true | all-gather | bytes 327680 | tf_op jit(solution)/shard_map/all_gather | solution.py:39
  41.1 2.8 convolution_convert_fusion.1
  46.5 2.8 reshape.137
  49.3 2.2 copy.52
  55.0 3.9 reshape.135
  58.9 3.3 copy.50
  62.2 2.8 fusion.63
  65.7 17.2 %all-gather.1 = bf16[32,64,64]{2,1,0:T(8,128)(2,1)} all-gather(bf16[8,64,64]{2,1,0:T(8,128)(2,1)S(1)} %convert_element_type.168), channel_id=3, replica_groups=mesh['grp'=2,'seq'=4,'outer'=4] {'seq'}, dimensions={0}, use_global_device_ids=true | all-gather | bytes 327680 | tf_op jit(solution)/shard_map/all_gather | solution.py:39
  82.9 30.7 %all-reduce.10 = (bf16[8,64,64]{2,1,0:T(8,128)(2,1)}, bf16[8,64,64]{2,1,0:T(8,128)(2,1)S(1)}) all-reduce(f32[8,64,64]{2,1,0:T(8,128)} %copy-done.15, f32[8,64,64]{2,1,0:T(8,128)S(1)} %get-tuple-element.351), channel_id=1, replica_groups=mesh['grp'=2,'seq'=4,'outer'=4] {'seq'}, use_global_device_ids=true, to_apply=%region_1.2 | all-reduce | flops 65536 | bytes 393216 | tf_op jit(solution)/shard_map/psum | solution.py:124
  113.6 7.2 %all-gather = bf16[32,64,64]{2,1,0:T(8,128)(2,1)} all-gather(bf16[8,64,64]{2,1,0:T(8,128)(2,1)} %get-tuple-element.338), channel_id=2, replica_groups=mesh['grp'=2,'seq'=4,'outer'=4] {'outer'}, dimensions={0}, use_global_device_ids=true | all-gather | bytes 327680 | tf_op jit(solution)/shard_map/all_gather | solution.py:39
  121.5 10.4 %all-gather.2 = bf16[32,64,64]{2,1,0:T(8,128)(2,1)} all-gather(bf16[8,64,64]{2,1,0:T(8,128)(2,1)S(1)} %get-tuple-element.339), channel_id=4, replica_groups=mesh['grp'=2,'seq'=4,'outer'=4] {'outer'}, dimensions={0}, use_global_device_ids=true | all-gather | bytes 327680 | tf_op jit(solution)/shard_map/all_gather | solution.py:39
  132.7 5.1 %while.60 = (s32[]{:T(128)}, f32[8,64,64]{2,1,0:T(8,128)}, s32[]{:T(128)}, bf16[4,8,64,64]{3,2,1,0:T(8,128)(2,1)}, s32[]{:T(128)}, /*index=5*/s32[]{:T(128)}, s32[]{:T(128)}, s32[]{:T(128)}) while((s32[]{:T(128)}, f32[8,64,64]{2,1,0:T(8,128)}, s32[]{:T(128)}, bf16[4,8,64,64]{3,2,1,0:T(8,128)(2,1)}, s32[]{:T(128)}, /*index=5*/s32[]{:T(128)}, ...), condition=%wide.region_10.11_spmd, body=%wide.region_9.10_spmd.sunk | while | flops 65542 | bytes 327823 | solution.py:46
  142.0 59.3 %while.62 = (s32[]{:T(128)}, bf16[2,512,512]{2,1,0:T(8,128)(2,1)}, bf16[2,512,512]{2,1,0:T(8,128)(2,1)}, bf16[2,512,512]{2,1,0:T(8,128)(2,1)}, bf16[2,512,8,64]{...) while((s32[]{:T(128)}, bf16[2,512,512]{2,1,0:T(8,128)(2,1)}, ...), condition=%wide.region_15.16_spmd, body=%wide.region_14.15_spmd.sunk | while | flops 1960837120 | bytes 65027896 | solution.py:132
  142.1 3.0 select_convert_fusion.6
  153.0 4.6 %fusion.130 = f32[8,64,512]{2,1,0:T(8,128)} fusion(f32[512]{0:T(512)S(1)} %bitcast.174, pred[512,512]{1,0:T(8,128)(4,1)S(1)} %iota_compare_fusion.2, bf16[2,512,8,64]{1,3,2,0:T(8,128)(2,1)} %get-tuple-element.651, s32[]{:T(128)S(6)} %copy.116, bf16[2,512,8,64]{1,3,2,0:T(8,128)(2,1)} %get-tuple-element.647, bf16[2,512,8,64]{1,3,2,0:T(8,128)(2,1)} %get-tuple-element.646), kind=kOutput, calls=%fused_computation.6.clone.1 | convolution fusion | flops 543162368 | bytes 2887168 | tf_op jit(solution)/shard_map/while/body/eval_jaxpr/hts,thj->shj/dot_general | solution.py:72
  157.7 2.9 fusion.131
  162.6 3.3 fusion.132
  169.4 2.2 constant_dynamic-update-slice_fusion.6
  171.8 3.0 select_convert_fusion.6
  182.7 4.6 %fusion.130 = f32[8,64,512]{2,1,0:T(8,128)} fusion(f32[512]{0:T(512)S(1)} %bitcast.174, pred[512,512]{1,0:T(8,128)(4,1)S(1)} %iota_compare_fusion.2, bf16[2,512,8,64]{1,3,2,0:T(8,128)(2,1)} %get-tuple-element.651, s32[]{:T(128)S(6)} %copy.116, bf16[2,512,8,64]{1,3,2,0:T(8,128)(2,1)} %get-tuple-element.647, bf16[2,512,8,64]{1,3,2,0:T(8,128)(2,1)} %get-tuple-element.646), kind=kOutput, calls=%fused_computation.6.clone.1 | convolution fusion | flops 543162368 | bytes 2887168 | tf_op jit(solution)/shard_map/while/body/eval_jaxpr/hts,thj->shj/dot_general | solution.py:72
  187.3 2.9 fusion.131
  192.3 3.3 fusion.132
  202.0 5.2 %collective-permute-start.2 = (bf16[3,512]{1,0:T(4,128)(2,1)S(1)}, bf16[3,512]{1,0:T(4,128)(2,1)S(1)}, u32[]{:S(2)}, u32[]{:S(2)}) collective-permute-start(bf16[3,512]{1,0:T(4,128)(2,1)S(1)} %slice.73), channel_id=1, source_target_pairs={{0,12},{4,0},{8,4},{12,8},{1,13},{5,1},{9,5},{13,9},{2,14},{6,2},{... | collective-permute-start | bytes 9224 | tf_op jit(solution)/shard_map/ppermute | solution.py:26
  207.3 3.0 convolution_bitcast_fusion.2
  217.7 68.8 %all-reduce.7.cloned.1.call-done = (f32[512,512]{0,1:T(8,128)}, f32[512,512]{0,1:T(8,128)}, f32[512,512]{0,1:T(8,128)}) async-done(((f32[512,512]{0,1:T(8,128)}, f32[512,512]{0,1:T(8,128)}, f32[512,512]{0,1:T(8,128)}), (f32[512,512]{0,1:T(8,128)}, f32[512,512]{0,1:T(8,128)}, f32[512,512]{0,1:T(8,128)})) %all-reduce.7.cloned.1.call-update) | async-done | bytes 3145744 | tf_op jit(solution)/shard_map/psum | solution.py:17
  286.6 2.3 fusion.51
  288.8 5.9 %psum.78 = f32[4,512]{1,0:T(4,128)S(1)} all-reduce(f32[4,512]{1,0:T(4,128)S(1)} %pad_maximum_fusion), channel_id=1, replica_groups=mesh['grp'=2,'seq'=4,'outer'=4] {'outer'}, use_global_device_ids=true, to_apply=%region_26.27 | all-reduce | flops 2048 | bytes 16384 | tf_op jit(solution)/shard_map/psum | solution.py:17
  294.7 13.4 %psum.79 = f32[4,512]{1,0:T(4,128)} all-reduce(f32[4,512]{1,0:T(4,128)S(1)} %psum.78), channel_id=1, replica_groups=mesh['grp'=2,'seq'=4,'outer'=4] {'seq'}, use_global_device_ids=true, to_apply=%region_27.28 | all-reduce | flops 2048 | bytes 16384 | tf_op jit(solution)/shard_map/psum | solution.py:17
  314.3 97.1 %all-reduce.9.cloned.1.call-done = (f32[512,512]{0,1:T(8,128)}, f32[512,512]{0,1:T(8,128)}, f32[512,512]{0,1:T(8,128)}) async-done(((f32[512,512]{0,1:T(8,128)}, f32[512,512]{0,1:T(8,128)}, f32[512,512]{0,1:T(8,128)}), (f32[512,512]{0,1:T(8,128)}, f32[512,512]{0,1:T(8,128)}, f32[512,512]{0,1:T(8,128)})) %all-reduce.9.cloned.1.call-update) | async-done | bytes 3145744 | tf_op jit(solution)/shard_map/psum | solution.py:17
  411.5 2.7 copy.57
  (160 shorter events, 76.7 us)
Async XLA Ops:
  7.2 6.1 %copy-start.18 = (bf16[1024,512]{1,0:T(8,128)(2,1)S(1)}, bf16[1024,512]{1,0:T(8,128)(2,1)}, u32[]{:S(2)}) copy-start(bf16[1024,512]{1,0:T(8,128)(2,1)} %param.17) | copy-start | bytes 3145732
  7.2 279.3 %all-reduce.7.cloned.1.call-start = ((), (), s32[]{:S(2)}) async-start(), calls=%async_computation | async-start | bytes 6291456 | tf_op jit(solution)/shard_map/psum | solution.py:17
  10.1 3.1 copy-start.17
  10.2 33.7 %collective-permute-start = (bf16[3,512]{1,0:T(4,128)(2,1)S(1)}, bf16[3,512]{1,0:T(4,128)(2,1)S(1)}, u32[]{:S(2)}, u32[]{:S(2)}) collective-permute-start(bf16[3,512]{1,0:T(4,128)(2,1)S(1)} %slice.65), channel_id=1, source_target_pairs={{0,4},{4,8},{8,12},{12,0},{1,5},{5,9},{9,13},{13,1},{2,6},{6,10},{... | collective-permute-start | bytes 9224 | tf_op jit(solution)/shard_map/ppermute | solution.py:26
  17.8 5.6 %copy-start.3 = (bf16[2,512,8,64]{1,3,2,0:T(8,128)(2,1)}, bf16[2,512,8,64]{1,3,2,0:T(8,128)(2,1)S(1)}, u32[]{:S(2)}) copy-start(bf16[2,512,8,64]{1,3,2,0:T(8,128)(2,1)S(1)} %copy.51) | copy-start | bytes 3145732
  17.9 5.3 %copy-start.24 = (f32[2,512]{1,0:T(2,128)}, f32[2,512]{1,0:T(2,128)S(1)}, u32[]{:S(2)}) copy-start(f32[2,512]{1,0:T(2,128)S(1)} %multiply_divide_fusion) | copy-start | bytes 12292
  25.6 57.3 %copy-start.13 = (f32[8,64,64]{2,1,0:T(8,128)}, f32[8,64,64]{2,1,0:T(8,128)S(1)}, u32[]{:S(2)}) copy-start(f32[8,64,64]{2,1,0:T(8,128)S(1)} %get-tuple-element.351) | copy-start | bytes 393220
  41.0 5.4 %copy-start.8 = (f32[8,64,64]{2,1,0:T(8,128)}, f32[8,64,64]{2,1,0:T(8,128)S(1)}, u32[]{:S(2)}) copy-start(f32[8,64,64]{2,1,0:T(8,128)S(1)} %get-tuple-element.225) | copy-start | bytes 393220
  41.0 4.1 copy-start.34
  43.9 7.6 %collective-permute-start.1 = (bf16[3,512]{1,0:T(4,128)(2,1)S(1)}, bf16[3,512]{1,0:T(4,128)(2,1)S(1)}, u32[]{:S(2)}, u32[]{:S(2)}) collective-permute-start(bf16[3,512]{1,0:T(4,128)(2,1)S(1)} %collective-permute-done), channel_id=1, source_target_pairs={{0,1},{1,2},{2,3},{4,5},{5,6},{6,7},{8,9},{9,10},{10,11},{12,13},{... | collective-permute-start | bytes 9224 | tf_op jit(solution)/shard_map/ppermute | solution.py:32
  45.2 7.9 %copy-start.26 = (f32[1,512]{1,0:T(1,128)}, f32[1,512]{1,0:T(1,128)S(1)}, u32[]{:S(2)}) copy-start(f32[1,512]{1,0:T(1,128)S(1)} %get-tuple-element.345) | copy-start | bytes 6148
  45.2 7.9 %copy-start.28 = (f32[1,512]{1,0:T(1,128)}, f32[1,512]{1,0:T(1,128)S(1)}, u32[]{:S(2)}) copy-start(f32[1,512]{1,0:T(1,128)S(1)} %get-tuple-element.346) | copy-start | bytes 6148
  45.2 7.9 %copy-start.30 = (f32[1,512]{1,0:T(1,128)}, f32[1,512]{1,0:T(1,128)S(1)}, u32[]{:S(2)}) copy-start(f32[1,512]{1,0:T(1,128)S(1)} %get-tuple-element.347) | copy-start | bytes 6148
  45.2 7.9 %copy-start.32 = (f32[1,512]{1,0:T(1,128)}, f32[1,512]{1,0:T(1,128)S(1)}, u32[]{:S(2)}) copy-start(f32[1,512]{1,0:T(1,128)S(1)} %get-tuple-element.348) | copy-start | bytes 6148
  137.8 3.3 copy-start.7
  137.8 3.3 copy-start.9
  137.8 3.3 copy-start.14
  137.8 3.3 copy-start.16
  138.9 3.1 copy-start.25
  142.1 3.0 copy-start.2
  145.1 2.5 copy-start.10
  162.6 3.3 copy-start.5
  162.6 3.3 copy-start.6
  171.8 3.0 copy-start.2
  192.3 3.3 copy-start.5
  192.3 3.3 copy-start.6
  202.0 8.3 %collective-permute-start.2 = (bf16[3,512]{1,0:T(4,128)(2,1)S(1)}, bf16[3,512]{1,0:T(4,128)(2,1)S(1)}, u32[]{:S(2)}, u32[]{:S(2)}) collective-permute-start(bf16[3,512]{1,0:T(4,128)(2,1)S(1)} %slice.73), channel_id=1, source_target_pairs={{0,12},{4,0},{8,4},{12,8},{1,13},{5,1},{9,5},{13,9},{2,14},{6,2},{... | collective-permute-start | bytes 9224 | tf_op jit(solution)/shard_map/ppermute | solution.py:26
  207.3 4.3 %copy-start.21 = (bf16[2,512,512]{2,1,0:T(8,128)(2,1)S(1)}, bf16[2,512,512]{2,1,0:T(8,128)(2,1)}, u32[]{:S(2)}) copy-start(bf16[2,512,512]{2,1,0:T(8,128)(2,1)} %get-tuple-element.228) | copy-start | bytes 3145732
  210.3 3.0 collective-permute-start.3
  217.7 193.8 %all-reduce.9.cloned.1.call-start = ((), (), s32[]{:S(2)}) async-start(), calls=%async_computation.1 | async-start | bytes 6291456 | tf_op jit(solution)/shard_map/psum | solution.py:17
  411.5 2.7 copy-start.20
  411.5 4.0 copy-start.19
  (15 other events, 22.4 us)
Sparse Core Ops, SparseCore 0:
  217.8 68.6 all-reduce.6
  289.1 122.3 all-reduce.8
